TPU v7x, 32 devices: a whole 2x2x4 slice. The times are simulated.
32 devices in a mesh: section: 2 (over x), space: 16 (over z, y, core).
Axes of the slice: x: 2, y: 2, z: 4, core: 2. Of those that a mesh axis runs over, the one named last changes fastest.
Arguments:
- input_tiles: bfloat16 [16, 2, 4, 8, 8, 256], P('space'), may hold values from -6 to 6
- saved_tiles: bfloat16 [16, 2, 32, 4, 4, 128], P('space'), may hold values from -6 to 6
- out_grad_tiles: bfloat16 [16, 2, 64, 2, 2, 64], P('space'), may hold values from -1 to 1
- kernel_first: bfloat16 [32, 4, 3, 3, 3], replicated, may hold values from -0.625 to 0.625
- bias_first: float32 [32], replicated, may hold values from -3 to 3
- kernel_second: bfloat16 [64, 32, 3, 3, 3], replicated, may hold values from -0.21875 to 0.21875
- bias_second: float32 [64], replicated, may hold values from -3 to 3
Outputs:
- grad_kernel_first: float32 [32, 4, 3, 3, 3], replicated
- grad_bias_first: float32 [32], replicated
- grad_kernel_second: float32 [64, 32, 3, 3, 3], replicated
- grad_bias_second: float32 [64], replicated
All inputs are finite; a program needn't handle non-finite values.
Results may differ from a plain program's by a relative error of at most 0.0031.
Values may be sent and summed in bfloat16 or wider, within the bound.
No kernel may reach another device: no remote copies, remote signals or barrier semaphores. Data moves between devices by JAX's collectives and lax.ppermute only.
A program may use at most 128 MiB of HBM per device.

v0:
```python
import jax
import jax.numpy as jnp
from jax import lax
from jax.sharding import PartitionSpec as P

GY = 8


def from_behind(value, axis, steps):
    count = lax.axis_size(axis)
    first, last = (max(0, -steps), min(count, count - steps))
    return lax.ppermute(value, axis, [(source, source + steps) for source in range(first, last)])


def correlate(padded, kernel):
    return lax.conv_general_dilated(
        padded,
        kernel,
        (1, 1, 1),
        "VALID",
        dimension_numbers=("NCDHW", "OIDHW", "NCDHW"),
        preferred_element_type=jnp.float32,
    )


def kernel_grad(padded, grads):
    result = lax.conv_general_dilated(
        padded,
        grads,
        (1, 1, 1),
        "VALID",
        dimension_numbers=("CNDHW", "IODHW", "NCDHW"),
        preferred_element_type=jnp.float32,
    )
    return jnp.transpose(result, (1, 0, 2, 3, 4))


def flipped(kernel):
    return jnp.transpose(kernel[:, :, ::-1, ::-1, ::-1], (1, 0, 2, 3, 4))


def spread_up(grad):
    batch, channels, rows_y, rows_z, rows_x = grad.shape
    value = grad.astype(jnp.float32) * 0.125
    value = jnp.broadcast_to(
        value[:, :, :, None, :, None, :, None], (batch, channels, rows_y, 2, rows_z, 2, rows_x, 2)
    )
    return value.reshape(batch, channels, 2 * rows_y, 2 * rows_z, 2 * rows_x)


def slope(pre):
    return jnp.where(pre > 0, 1.0, 0.3)


def bias_column(bias):
    return bias[None, :, None, None, None]


def widen_last(field):
    return jnp.pad(field, ((0, 0), (0, 0), (0, 0), (0, 0), (1, 1)))


def extend(field):
    grid_z = lax.axis_size("space") // GY
    place = lax.axis_index("space") % grid_z
    last_plane = field[:, :, :, -1:]
    first_plane = field[:, :, :, :1]
    last_plane = jnp.where(place < grid_z - 1, last_plane, jnp.zeros_like(last_plane))
    first_plane = jnp.where(place > 0, first_plane, jnp.zeros_like(first_plane))
    low_z = from_behind(last_plane, "space", 1)
    high_z = from_behind(first_plane, "space", -1)
    wide = jnp.concatenate([low_z, field, high_z], axis=3)
    low_y = from_behind(wide[:, :, -1:], "space", grid_z)
    high_y = from_behind(wide[:, :, :1], "space", -grid_z)
    return widen_last(jnp.concatenate([low_y, wide, high_y], axis=2))


def second_delta(second_ext, cotangent, kernel_second, bias_second):
    pre_two = correlate(second_ext, kernel_second) + bias_column(bias_second)
    return (spread_up(cotangent) * slope(pre_two)).astype(jnp.bfloat16)


def first_grads(first_ext, arrived, kernel_first, bias_first):
    pre_one = correlate(first_ext, kernel_first) + bias_column(bias_first)
    delta_one = (spread_up(arrived) * slope(pre_one)).astype(jnp.bfloat16)
    return (
        kernel_grad(first_ext, delta_one),
        jnp.sum(delta_one, axis=(0, 2, 3, 4), dtype=jnp.float32),
    )


def on_device(
    input_tiles, saved_tiles, out_grad_tiles, kernel_first, bias_first, kernel_second, bias_second
):
    first = input_tiles[0]
    second = saved_tiles[0]
    cotangent = out_grad_tiles[0]
    section = lax.axis_index("section")
    batches = first.shape[0]
    flipped_two = flipped(kernel_second)
    share = batches // lax.axis_size("section")
    offset = section * share
    local_first = lax.dynamic_slice_in_dim(first, offset, share, 0)
    local_second = lax.dynamic_slice_in_dim(second, offset, share, 0)
    local_cot = lax.dynamic_slice_in_dim(cotangent, offset, share, 0)
    second_ext = extend(local_second)
    first_ext = extend(local_first)
    delta_two = second_delta(second_ext, local_cot, kernel_second, bias_second)
    delta_ext = extend(delta_two)
    grad_w_two = kernel_grad(second_ext, delta_two)
    grad_b_two = jnp.sum(delta_two, axis=(0, 2, 3, 4), dtype=jnp.float32)
    back = correlate(delta_ext, flipped_two).astype(jnp.bfloat16)
    grad_w_one, grad_b_one = first_grads(first_ext, back, kernel_first, bias_first)
    total = lax.psum((grad_w_one, grad_b_one, grad_w_two, grad_b_two), ("section", "space"))
    return (total[0], total[1], total[2], total[3])


def solution(mesh):
    placed = (
        P("space", None, None, None, None, None),
        P("space", None, None, None, None, None),
        P("space", None, None, None, None, None),
        P(),
        P(),
        P(),
        P(),
    )
    return jax.shard_map(
        on_device, mesh=mesh, in_specs=placed, out_specs=(P(), P(), P(), P()), check_vma=False
    )
```

profile of v0, /device:TPU:0, one launch (start us, length us, event | category | flops | bytes accessed | tf_op | source)
XLA Modules:
  0.0 405.5 jit_solution(2935043332899590350)
XLA Ops:
  8.2 2.4 collective-permute-start
  13.0 5.2 %collective-permute-start.4 = (bf16[1,32,4,1,128]{4,1,3,2,0:T(8,128)(2,1)S(1)}, bf16[1,32,4,1,128]{4,1,3,2,0:T(8,128)(2,1)S(1)}, u32[]{:S(2)}, u32[]{:S(2)}) collective-permute-start(bf16[1,32,4,1,128]{4,1,3,2,0:T(8,128)(2,1)S(1)} %get-tuple-element.19), channel_id=1, source_target_pairs={{0,1},{1,2},{2,3},{3,4},{4,5},{5,6},{6,7},{7,8},{8,9},{9,10},{10,1... | collective-permute-start | bytes 98312 | tf_op jit(solution)/shard_map/ppermute | solution.py:12
  20.3 9.1 %copy.94 = bf16[1,4,8,8,256]{1,0,4,3,2:T(2,128)(2,1)} copy(bf16[1,4,8,8,256]{4,3,2,1,0:T(8,128)(2,1)S(1)} %dynamic-slice_bitcast_fusion) | data formatting | bytes 262144 | tf_op jit(solution)/shard_map/dynamic_slice | solution.py:103
  30.8 7.0 %pad_maximum_fusion.3 = (bf16[1,4,1,10,256]{1,0,4,3,2:T(2,128)(2,1)}, bf16[1,4,1,10,256]{1,0,4,3,2:T(2,128)(2,1)}) fusion(bf16[1,4,8,1,256]{1,0,4,3,2:T(2,128)(2,1)S(1)} %copy.95, bf16[1,4,8,8,256]{1,0,4,3,2:T(2,128)(2,1)} %copy.94, bf16[1,4,8,1,256]{1,0,4,3,2:T(2,128)(2,1)S(1)} %copy.93), kind=kLoop, calls=%fused_computation.43 | loop fusion | flops 40960 | bytes 204800 | tf_op jit(solution)/shard_map/slice | solution.py:73
  37.9 2.5 copy.96
  40.4 5.9 %collective-permute-start.2 = (bf16[1,4,1,10,256]{4,1,3,2,0:T(4,128)(2,1)S(1)}, bf16[1,4,1,10,256]{4,1,3,2,0:T(4,128)(2,1)S(1)}, u32[]{:S(2)}, u32[]{:S(2)}) collective-permute-start(bf16[1,4,1,10,256]{4,1,3,2,0:T(4,128)(2,1)S(1)} %copy.96), channel_id=1, source_target_pairs={{0,2},{1,3},{2,4},{3,5},{4,6},{5,7},{6,8},{7,9},{8,10},{9,11},{10,... | collective-permute-start | bytes 61448 | tf_op jit(solution)/shard_map/ppermute | solution.py:12
  46.3 2.5 copy.97
  50.1 5.9 %collective-permute-start.6 = (bf16[1,32,1,6,128]{4,1,3,2,0:T(8,128)(2,1)S(1)}, bf16[1,32,1,6,128]{4,1,3,2,0:T(8,128)(2,1)S(1)}, u32[]{:S(2)}, u32[]{:S(2)}) collective-permute-start(bf16[1,32,1,6,128]{4,1,3,2,0:T(8,128)(2,1)S(1)} %get-tuple-element.17), channel_id=1, source_target_pairs={{0,2},{1,3},{2,4},{3,5},{4,6},{5,7},{6,8},{7,9},{8,10},{9,11},{10,... | collective-permute-start | bytes 147464 | tf_op jit(solution)/shard_map/ppermute | solution.py:12
  56.0 1.5 collective-permute-start.7
  57.5 2.2 copy.98
  59.7 2.2 copy.99
  61.8 40.1 %pad_maximum_fusion = bf16[1,4,10,10,256]{1,0,4,3,2:T(2,128)(2,1)} fusion(bf16[1,4,1,10,256]{1,0,4,3,2:T(2,128)(2,1)} %copy.99, bf16[1,4,8,1,256]{1,0,4,3,2:T(2,128)(2,1)S(1)} %copy.95, bf16[1,4,8,8,256]{1,0,4,3,2:T(2,128)(2,1)} %copy.94, bf16[1,4,8,1,256]{1,0,4,3,2:T(2,128)(2,1)S(1)} %copy.93, bf16[1,4,1,10,256]{1,0,4,3,2:T(2,128)(2,1)} %copy.98), kind=kLoop, calls=%fused_computation | loop fusion | flops 409600 | bytes 409600 | tf_op jit(solution)/shard_map/concatenate | solution.py:75
  101.9 23.7 %copy.113 = bf16[1,4,10,10,256]{4,1,3,2,0:T(4,128)(2,1)S(1)} copy(bf16[1,4,10,10,256]{1,0,4,3,2:T(2,128)(2,1)} %pad_maximum_fusion) | data formatting | bytes 409600 | tf_op jit(solution)/shard_map/concatenate | solution.py:75
  126.6 4.3 %copy.115 = bf16[4,10,10,1,8,33]{4,0,5,2,1,3:T(4,128)(2,1)} copy(bf16[4,10,10,1,8,33]{5,4,0,2,1,3:T(8,128)(2,1)S(1)} %reshape.57) | data formatting | bytes 422400 | tf_op jit(solution)/shard_map/conv_general_dilated | solution.py:16
  132.1 20.5 %fusion = f32[8,8,8,33,32]{4,2,3,1,0:T(8,128)S(1)} fusion(f32[32]{0:T(128)S(1)} %copy-done.9, pred[8,33]{0,1:T(8,128)(4,1)S(1)} %copy-done.11, bf16[32,4,3,3,3]{0,1,4,3,2:T(4,128)(2,1)S(1)} %copy-done.8, bf16[4,10,10,1,7,2]{4,0,5,2,1,3:T(4,128)(2,1)S(1)} %slice.64, bf16[4,10,10,1,8,33]{4,0,5,2,1,3:T(4,128)(2,1)} %copy.115), kind=kOutput, calls=%fused_computation.2 | convolution fusion | flops 119619840 | bytes 2392392 | tf_op jit(solution)/shard_map/conv_general_dilated | solution.py:16
  152.6 6.0 %copy.121 = f32[8,8,8,33,32]{4,3,2,1,0:T(8,128)} copy(f32[8,8,8,33,32]{4,2,3,1,0:T(8,128)S(1)} %fusion) | data formatting | bytes 4325376 | tf_op jit(solution)/shard_map/jit(_where)/select_n | solution.py:52
  158.6 9.5 %reshape.76 = f32[8,8,1,264,32]{4,3,1,0,2:T(8,128)} reshape(f32[8,8,8,33,32]{4,3,2,1,0:T(8,128)} %copy.121) | data formatting | bytes 4325376 | tf_op jit(solution)/shard_map/jit(_where)/select_n | solution.py:52
  169.0 1.7 reshape.45
  170.8 3.0 copy.103
  174.8 3.5 fusion.53
  180.0 1.4 broadcast_select_fusion.1
  181.6 2.0 collective-permute-start.8
  185.7 4.7 %copy.119 = bf16[1,32,6,6,128]{1,0,4,3,2:T(2,128)(2,1)S(1)} copy(bf16[1,32,6,6,128]{4,1,3,2,0:T(8,128)(2,1)} %pad_maximum_fusion.4) | data formatting | bytes 589824 | tf_op jit(solution)/shard_map/concatenate | solution.py:75
  193.2 7.7 %collective-permute-start.10 = (bf16[1,64,1,6,128]{4,1,3,2,0:T(8,128)(2,1)}, bf16[1,64,1,6,128]{4,1,3,2,0:T(8,128)(2,1)S(1)}, u32[]{:S(2)}, u32[]{:S(2)}) collective-permute-start(bf16[1,64,1,6,128]{4,1,3,2,0:T(8,128)(2,1)} %get-tuple-element.15), channel_id=1, source_target_pairs={{0,2},{1,3},{2,4},{3,5},{4,6},{5,7},{6,8},{7,9},{8,10},{9,11},{10,... | collective-permute-start | bytes 294920 | tf_op jit(solution)/shard_map/ppermute | solution.py:12
  201.0 1.5 collective-permute-start.11
  202.4 14.7 %fusion.58 = f32[64,32,3,3,3]{0,1,4,3,2:T(8,128)} fusion(bf16[1,32,6,6,128]{1,0,4,3,2:T(2,128)(2,1)S(1)} %copy.119, bf16[1,64,4,4,128]{1,3,4,2,0:T(4,128)(2,1)S(1)} %get-tuple-element.8), kind=kOutput, calls=%fused_computation.50 | convolution fusion | flops 225312768 | bytes 778240 | tf_op jit(solution)/shard_map/transpose | solution.py:35
  220.7 4.3 %fusion.50 = f32[4,4,8,17,32]{4,2,3,1,0:T(8,128)S(1)} fusion(bf16[64,32,3,3,3]{0,1,4,3,2:T(8,128)(2,1)S(1)} %copy-done.7, bf16[64,6,6,1,7,2]{0,4,5,2,1,3:T(8,128)(2,1)S(1)} %slice.62, bf16[64,6,6,1,8,17]{0,4,5,2,1,3:T(8,128)(2,1)S(1)} %copy.110, pred[8,17]{0,1:T(8,128)(4,1)S(1)} %copy-done.12), kind=kOutput, calls=%fused_computation.40 | convolution fusion | flops 243027968 | bytes 1080456 | tf_op jit(solution)/shard_map/conv_general_dilated | solution.py:16
  225.6 7.3 %broadcast_in_dim.41 = f32[32,4,2,4,2,128,2]{0,6,5,4,3,2,1:T(2,128)} broadcast(f32[32,4,4,128]{0,3,2,1:T(8,128)S(1)} %copy.112), dimensions={0,1,3,5} | broadcast | bytes 2359296 | tf_op jit(solution)/shard_map/broadcast_in_dim | solution.py:45
  232.9 7.6 %convert_reduce_fusion = (f32[32]{0:T(128)}, bf16[1,32,8,8,256]{1,4,3,2,0:T(8,128)(2,1)S(1)}) fusion(f32[1,32,8,8,256]{1,4,3,2,0:T(8,128)} %bitcast.76, f32[8,8,1,264,32]{4,3,1,0,2:T(8,128)} %reshape.76), kind=kLoop, calls=%fused_computation.6 | loop fusion | flops 2097120 | bytes 5243008 | tf_op jit(solution)/shard_map/reduce_sum | solution.py:88
  240.5 111.0 %fusion.3 = f32[32,4,3,3,3]{0,1,4,3,2:T(4,128)S(1)} fusion(bf16[1,4,10,10,256]{1,0,4,3,2:T(2,128)(2,1)} %pad_maximum_fusion, bf16[1,32,8,8,256]{1,4,3,2,0:T(8,128)(2,1)S(1)} %get-tuple-element.10), kind=kOutput, calls=%fused_computation.7 | convolution fusion | flops 112951296 | bytes 1267200 | tf_op jit(solution)/shard_map/transpose | solution.py:35
  351.5 44.9 %all-reduce = (f32[32,4,3,3,3]{0,1,4,3,2:T(4,128)}, f32[32]{0:T(128)}, f32[64]{0:T(128)}) all-reduce(f32[32,4,3,3,3]{0,1,4,3,2:T(4,128)S(1)} %fusion.3, f32[32]{0:T(128)S(1)} %copy-done.4, f32[64]{0:T(128)S(1)} %copy-done.5), channel_id=1, replica_groups=mesh['section'=2,'space'=16] {'section','space'}, use_global_device_ids=true, to_apply=%region_0.1 | all-reduce | flops 3552 | bytes 28416 | tf_op jit(solution)/shard_map/psum | solution.py:114
  396.4 1.8 copy.132
  (80 shorter events, 22.9 us)
Async XLA Ops:
  7.2 1.0 copy-start
  7.2 389.2 %all-reduce.3.cloned.1.call-start = ((), (), s32[]{:S(2)}) async-start(), calls=%async_computation | async-start | bytes 884736 | tf_op jit(solution)/shard_map/psum | solution.py:114
  8.2 21.3 %collective-permute-start = (bf16[1,4,8,1,256]{4,2,3,1,0:T(8,128)(2,1)S(1)}, bf16[1,4,8,1,256]{4,2,3,1,0:T(8,128)(2,1)S(1)}, u32[]{:S(2)}, u32[]{:S(2)}) collective-permute-start(bf16[1,4,8,1,256]{4,2,3,1,0:T(8,128)(2,1)S(1)} %copy.91), channel_id=1, source_target_pairs={{0,1},{1,2},{2,3},{3,4},{4,5},{5,6},{6,7},{7,8},{8,9},{9,10},{10,1... | collective-permute-start | bytes 49160 | tf_op jit(solution)/shard_map/ppermute | solution.py:12
  10.7 19.5 %collective-permute-start.1 = (bf16[1,4,8,1,256]{4,2,3,1,0:T(8,128)(2,1)S(1)}, bf16[1,4,8,1,256]{4,2,3,1,0:T(8,128)(2,1)S(1)}, u32[]{:S(2)}, u32[]{:S(2)}) collective-permute-start(bf16[1,4,8,1,256]{4,2,3,1,0:T(8,128)(2,1)S(1)} %copy.92), channel_id=1, source_target_pairs={{1,0},{2,1},{3,2},{4,3},{5,4},{6,5},{7,6},{8,7},{9,8},{10,9},{11,1... | collective-permute-start | bytes 49160 | tf_op jit(solution)/shard_map/ppermute | solution.py:12
  13.0 37.1 %collective-permute-start.4 = (bf16[1,32,4,1,128]{4,1,3,2,0:T(8,128)(2,1)S(1)}, bf16[1,32,4,1,128]{4,1,3,2,0:T(8,128)(2,1)S(1)}, u32[]{:S(2)}, u32[]{:S(2)}) collective-permute-start(bf16[1,32,4,1,128]{4,1,3,2,0:T(8,128)(2,1)S(1)} %get-tuple-element.19), channel_id=1, source_target_pairs={{0,1},{1,2},{2,3},{3,4},{4,5},{5,6},{6,7},{7,8},{8,9},{9,10},{10,1... | collective-permute-start | bytes 98312 | tf_op jit(solution)/shard_map/ppermute | solution.py:12
  18.1 32.0 %collective-permute-start.5 = (bf16[1,32,4,1,128]{4,1,3,2,0:T(8,128)(2,1)S(1)}, bf16[1,32,4,1,128]{4,1,3,2,0:T(8,128)(2,1)S(1)}, u32[]{:S(2)}, u32[]{:S(2)}) collective-permute-start(bf16[1,32,4,1,128]{4,1,3,2,0:T(8,128)(2,1)S(1)} %get-tuple-element.20), channel_id=1, source_target_pairs={{1,0},{2,1},{3,2},{4,3},{5,4},{6,5},{7,6},{8,7},{9,8},{10,9},{11,1... | collective-permute-start | bytes 98312 | tf_op jit(solution)/shard_map/ppermute | solution.py:12
  40.4 17.1 %collective-permute-start.2 = (bf16[1,4,1,10,256]{4,1,3,2,0:T(4,128)(2,1)S(1)}, bf16[1,4,1,10,256]{4,1,3,2,0:T(4,128)(2,1)S(1)}, u32[]{:S(2)}, u32[]{:S(2)}) collective-permute-start(bf16[1,4,1,10,256]{4,1,3,2,0:T(4,128)(2,1)S(1)} %copy.96), channel_id=1, source_target_pairs={{0,2},{1,3},{2,4},{3,5},{4,6},{5,7},{6,8},{7,9},{8,10},{9,11},{10,... | collective-permute-start | bytes 61448 | tf_op jit(solution)/shard_map/ppermute | solution.py:12
  48.8 10.9 %collective-permute-start.3 = (bf16[1,4,1,10,256]{4,1,3,2,0:T(4,128)(2,1)S(1)}, bf16[1,4,1,10,256]{4,1,3,2,0:T(4,128)(2,1)S(1)}, u32[]{:S(2)}, u32[]{:S(2)}) collective-permute-start(bf16[1,4,1,10,256]{4,1,3,2,0:T(4,128)(2,1)S(1)} %copy.97), channel_id=1, source_target_pairs={{2,0},{3,1},{4,2},{5,3},{6,4},{7,5},{8,6},{9,7},{10,8},{11,9},{12,... | collective-permute-start | bytes 61448 | tf_op jit(solution)/shard_map/ppermute | solution.py:12
  50.1 118.0 %collective-permute-start.6 = (bf16[1,32,1,6,128]{4,1,3,2,0:T(8,128)(2,1)S(1)}, bf16[1,32,1,6,128]{4,1,3,2,0:T(8,128)(2,1)S(1)}, u32[]{:S(2)}, u32[]{:S(2)}) collective-permute-start(bf16[1,32,1,6,128]{4,1,3,2,0:T(8,128)(2,1)S(1)} %get-tuple-element.17), channel_id=1, source_target_pairs={{0,2},{1,3},{2,4},{3,5},{4,6},{5,7},{6,8},{7,9},{8,10},{9,11},{10,... | collective-permute-start | bytes 147464 | tf_op jit(solution)/shard_map/ppermute | solution.py:12
  56.0 112.2 %collective-permute-start.7 = (bf16[1,32,1,6,128]{4,1,3,2,0:T(8,128)(2,1)S(1)}, bf16[1,32,1,6,128]{4,1,3,2,0:T(8,128)(2,1)S(1)}, u32[]{:S(2)}, u32[]{:S(2)}) collective-permute-start(bf16[1,32,1,6,128]{4,1,3,2,0:T(8,128)(2,1)S(1)} %get-tuple-element.18), channel_id=1, source_target_pairs={{2,0},{3,1},{4,2},{5,3},{6,4},{7,5},{8,6},{9,7},{10,8},{11,9},{12,... | collective-permute-start | bytes 147464 | tf_op jit(solution)/shard_map/ppermute | solution.py:12
  126.6 5.5 %copy-start.8 = (bf16[32,4,3,3,3]{0,1,4,3,2:T(4,128)(2,1)S(1)}, bf16[32,4,3,3,3]{0,1,4,3,2:T(4,128)(2,1)}, u32[]{:S(2)}) copy-start(bf16[32,4,3,3,3]{0,1,4,3,2:T(4,128)(2,1)} %param.10) | copy-start | bytes 20740
  126.6 5.5 %copy-start.9 = (f32[32]{0:T(128)S(1)}, f32[32]{0:T(128)}, u32[]{:S(2)}) copy-start(f32[32]{0:T(128)} %param.11) | copy-start | bytes 388
  126.6 5.5 %copy-start.11 = (pred[8,33]{0,1:T(8,128)(4,1)S(1)}, pred[8,33]{0,1:T(8,128)(4,1)}, u32[]{:S(2)}) copy-start(pred[8,33]{0,1:T(8,128)(4,1)} %constant.64) | copy-start | bytes 796
  168.2 0.6 copy-start.2
  170.8 4.0 copy-start.6
  170.8 4.0 copy-start.10
  170.8 4.0 copy-start.12
  178.9 6.1 %copy-start.3 = (bf16[1,32,1,6,128]{4,1,3,2,0:T(8,128)(2,1)S(1)}, bf16[1,32,1,6,128]{4,1,3,2,0:T(8,128)(2,1)}, u32[]{:S(2)}) copy-start(bf16[1,32,1,6,128]{4,1,3,2,0:T(8,128)(2,1)} %copy-done.2) | copy-start | bytes 147460
  181.6 8.8 %collective-permute-start.8 = (bf16[1,64,4,1,128]{1,3,4,2,0:T(2,128)(2,1)}, bf16[1,64,4,1,128]{1,3,4,2,0:T(2,128)(2,1)}, u32[]{:S(2)}, u32[]{:S(2)}) collective-permute-start(bf16[1,64,4,1,128]{1,3,4,2,0:T(2,128)(2,1)} %get-tuple-element.13), channel_id=1, source_target_pairs={{0,1},{1,2},{2,3},{3,4},{4,5},{5,6},{6,7},{7,8},{8,9},{9,10},{10,1... | collective-permute-start | bytes 196616 | tf_op jit(solution)/shard_map/ppermute | solution.py:12
  183.6 7.8 %collective-permute-start.9 = (bf16[1,64,4,1,128]{1,3,4,2,0:T(2,128)(2,1)}, bf16[1,64,4,1,128]{1,3,4,2,0:T(2,128)(2,1)}, u32[]{:S(2)}, u32[]{:S(2)}) collective-permute-start(bf16[1,64,4,1,128]{1,3,4,2,0:T(2,128)(2,1)} %get-tuple-element.14), channel_id=1, source_target_pairs={{1,0},{2,1},{3,2},{4,3},{5,4},{6,5},{7,6},{8,7},{9,8},{10,9},{11,1... | collective-permute-start | bytes 196616 | tf_op jit(solution)/shard_map/ppermute | solution.py:12
  193.2 24.0 %collective-permute-start.10 = (bf16[1,64,1,6,128]{4,1,3,2,0:T(8,128)(2,1)}, bf16[1,64,1,6,128]{4,1,3,2,0:T(8,128)(2,1)S(1)}, u32[]{:S(2)}, u32[]{:S(2)}) collective-permute-start(bf16[1,64,1,6,128]{4,1,3,2,0:T(8,128)(2,1)} %get-tuple-element.15), channel_id=1, source_target_pairs={{0,2},{1,3},{2,4},{3,5},{4,6},{5,7},{6,8},{7,9},{8,10},{9,11},{10,... | collective-permute-start | bytes 294920 | tf_op jit(solution)/shard_map/ppermute | solution.py:12
  201.0 16.2 %collective-permute-start.11 = (bf16[1,64,1,6,128]{4,1,3,2,0:T(8,128)(2,1)S(1)}, bf16[1,64,1,6,128]{4,1,3,2,0:T(8,128)(2,1)}, u32[]{:S(2)}, u32[]{:S(2)}) collective-permute-start(bf16[1,64,1,6,128]{4,1,3,2,0:T(8,128)(2,1)S(1)} %get-tuple-element.16), channel_id=1, source_target_pairs={{2,0},{3,1},{4,2},{5,3},{6,4},{7,5},{8,6},{9,7},{10,8},{11,9},{12,... | collective-permute-start | bytes 294920 | tf_op jit(solution)/shard_map/ppermute | solution.py:12
  219.8 0.9 copy-start.7
  240.5 111.0 %copy-start.4 = (f32[32]{0:T(128)S(1)}, f32[32]{0:T(128)}, u32[]{:S(2)}) copy-start(f32[32]{0:T(128)} %get-tuple-element.9) | copy-start | bytes 388
  240.5 111.0 %copy-start.5 = (f32[64]{0:T(128)S(1)}, f32[64]{0:T(128)}, u32[]{:S(2)}) copy-start(f32[64]{0:T(128)} %get-tuple-element.7) | copy-start | bytes 772
  240.5 157.7 %copy-start.1 = (bf16[1,2,4,8,8,256]{5,4,3,2,1,0:T(8,128)(2,1)S(1)}, bf16[1,2,4,8,8,256]{5,4,3,2,1,0:T(8,128)(2,1)}, u32[]{:S(2)}) copy-start(bf16[1,2,4,8,8,256]{5,4,3,2,1,0:T(8,128)(2,1)} %param.7) | copy-start | bytes 786436
Sparse Core Ops, SparseCore 0:
  217.3 131.7 all-reduce.2
where the time goes:
time: 411 us; the launch traced here: 406 us
  matrix products  154 us (37%)
  local copies, waits for them, and re-layouts  93.5 us (23%)
  other arithmetic  60.7 us (15%)
  blocking collectives  44.9 us (11%)
  starting transfers between devices  37.2 us (9%)
  between operations  15.1 us (4%)
    transpose x2, matrix products, kernel_grad(): return jnp.transpose(result, (1, 0, 2, 3, 4))  126 us
    psum x1, blocking collectives, on_device(): lax.psum((grad_w_one, grad_b_one, grad_w_two, grad_b_two), ('section', 's...  44.9 us
    concatenate x4, other arithmetic, extend(): return widen_last(jnp.concatenate([low_y, wide, high_y], axis=2))  41.9 us
    ppermute x12, starting transfers between devices, from_behind(): lax.ppermute(value, axis, [(source, source + steps) for source in range(f...  37.2 us
    concatenate x5, local copies, waits for them, and re-layouts, extend(): return widen_last(jnp.concatenate([low_y, wide, high_y], axis=2))  29.2 us
    conv_general_dilated x3, matrix products, correlate(): lax.conv_general_dilated(padded, kernel, (1, 1, 1), 'VALID', dimension_nu...  28.4 us
    select_n x3, local copies, waits for them, and re-layouts, slope(): return jnp.where(pre > 0, 1.0, 0.3)  15.8 us
    conv_general_dilated x9, local copies, waits for them, and re-layouts, correlate(): lax.conv_general_dilated(padded, kernel, (1, 1, 1), 'VALID', dimension_nu...  12.5 us
  transfers between devices with their start and end apart: 13, of which 0 were waited for; matrix products, arithmetic and copies ran while one was open for 71% of the time, Pallas kernels for 0%

commit v1 on v0

--- a/solution.py
+++ b/solution.py
@@ -111,7 +111,8 @@
     grad_b_two = jnp.sum(delta_two, axis=(0, 2, 3, 4), dtype=jnp.float32)
     back = correlate(delta_ext, flipped_two).astype(jnp.bfloat16)
     grad_w_one, grad_b_one = first_grads(first_ext, back, kernel_first, bias_first)
-    total = lax.psum((grad_w_one, grad_b_one, grad_w_two, grad_b_two), ("section", "space"))
+    partial = lax.psum((grad_w_one, grad_b_one, grad_w_two, grad_b_two), "section")
+    total = lax.psum(partial, "space")
     return (total[0], total[1], total[2], total[3])
 
 

time: 411 us -> 428 us (1.041)
  blocking collectives: 44.9 us -> 67.7 us
  matrix products: 154 us -> 140 us
  waiting for transfers between devices: 0.05 us -> 6.36 us
    psum x1 -> x2, blocking collectives: 44.9 us -> 67.7 us  [the longest x1 60.1 us: on_device(): total = lax.psum(partial, 'space')]
    transpose x2, matrix products: 126 us -> 112 us  [kernel_grad(): return jnp.transpose(result, (1, 0, 2, 3, 4))]
    psum x1 -> x2, waiting for transfers between devices: 0.01 us -> 6.3 us  [the longest x1 6.3 us: on_device(): lax.psum((grad_w_one, grad_b_one, grad_w_two, grad_b_two), 'section')]
  transfers between devices with their start and end apart: 13 -> 14, of which waited for: 0 -> 1; matrix products, arithmetic and copies ran while one was open for 71% -> 66% of each run, Pallas kernels for 0% -> 0%
where the time goes in v1:
time: 428 us; the launch traced here: 423 us
  matrix products  140 us (33%)
  local copies, waits for them, and re-layouts  93.6 us (22%)
  blocking collectives  67.7 us (16%)
  other arithmetic  62.7 us (15%)
  starting transfers between devices  37.2 us (9%)
  between operations  15.1 us (4%)
  waiting for transfers between devices  6.36 us (1%)
    transpose x2, matrix products, kernel_grad(): return jnp.transpose(result, (1, 0, 2, 3, 4))  112 us
    psum x1, blocking collectives, on_device(): total = lax.psum(partial, 'space')  60.1 us
    concatenate x4, other arithmetic, extend(): return widen_last(jnp.concatenate([low_y, wide, high_y], axis=2))  41.9 us
    ppermute x12, starting transfers between devices, from_behind(): lax.ppermute(value, axis, [(source, source + steps) for source in range(f...  37.2 us
    concatenate x5, local copies, waits for them, and re-layouts, extend(): return widen_last(jnp.concatenate([low_y, wide, high_y], axis=2))  29.2 us
    conv_general_dilated x3, matrix products, correlate(): lax.conv_general_dilated(padded, kernel, (1, 1, 1), 'VALID', dimension_nu...  28.3 us
    select_n x3, local copies, waits for them, and re-layouts, slope(): return jnp.where(pre > 0, 1.0, 0.3)  15.9 us
    conv_general_dilated x9, local copies, waits for them, and re-layouts, correlate(): lax.conv_general_dilated(padded, kernel, (1, 1, 1), 'VALID', dimension_nu...  12.5 us
  transfers between devices with their start and end apart: 14, of which 1 were waited for; matrix products, arithmetic and copies ran while one was open for 66% of the time, Pallas kernels for 0%

profile of v1, /device:TPU:0, one launch (start us, length us, event | category | flops | bytes accessed | tf_op | source)
XLA Modules:
  0.0 423.2 jit_solution(1498709366230446219)
XLA Ops:
  8.2 2.4 collective-permute-start
  13.0 5.2 %collective-permute-start.4 = (bf16[1,32,4,1,128]{4,1,3,2,0:T(8,128)(2,1)S(1)}, bf16[1,32,4,1,128]{4,1,3,2,0:T(8,128)(2,1)S(1)}, u32[]{:S(2)}, u32[]{:S(2)}) collective-permute-start(bf16[1,32,4,1,128]{4,1,3,2,0:T(8,128)(2,1)S(1)} %get-tuple-element.22), channel_id=1, source_target_pairs={{0,1},{1,2},{2,3},{3,4},{4,5},{5,6},{6,7},{7,8},{8,9},{9,10},{10,1... | collective-permute-start | bytes 98312 | tf_op jit(solution)/shard_map/ppermute | solution.py:12
  20.3 9.1 %copy.94 = bf16[1,4,8,8,256]{1,0,4,3,2:T(2,128)(2,1)} copy(bf16[1,4,8,8,256]{4,3,2,1,0:T(8,128)(2,1)S(1)} %dynamic-slice_bitcast_fusion) | data formatting | bytes 262144 | tf_op jit(solution)/shard_map/dynamic_slice | solution.py:103
  30.9 7.1 %pad_maximum_fusion.3 = (bf16[1,4,1,10,256]{1,0,4,3,2:T(2,128)(2,1)}, bf16[1,4,1,10,256]{1,0,4,3,2:T(2,128)(2,1)}) fusion(bf16[1,4,8,1,256]{1,0,4,3,2:T(2,128)(2,1)S(1)} %copy.95, bf16[1,4,8,8,256]{1,0,4,3,2:T(2,128)(2,1)} %copy.94, bf16[1,4,8,1,256]{1,0,4,3,2:T(2,128)(2,1)S(1)} %copy.93), kind=kLoop, calls=%fused_computation.43 | loop fusion | flops 40960 | bytes 204800 | tf_op jit(solution)/shard_map/slice | solution.py:73
  37.9 2.5 copy.96
  40.4 5.9 %collective-permute-start.2 = (bf16[1,4,1,10,256]{4,1,3,2,0:T(4,128)(2,1)S(1)}, bf16[1,4,1,10,256]{4,1,3,2,0:T(4,128)(2,1)S(1)}, u32[]{:S(2)}, u32[]{:S(2)}) collective-permute-start(bf16[1,4,1,10,256]{4,1,3,2,0:T(4,128)(2,1)S(1)} %copy.96), channel_id=1, source_target_pairs={{0,2},{1,3},{2,4},{3,5},{4,6},{5,7},{6,8},{7,9},{8,10},{9,11},{10,... | collective-permute-start | bytes 61448 | tf_op jit(solution)/shard_map/ppermute | solution.py:12
  46.3 2.5 copy.97
  50.2 5.9 %collective-permute-start.6 = (bf16[1,32,1,6,128]{4,1,3,2,0:T(8,128)(2,1)S(1)}, bf16[1,32,1,6,128]{4,1,3,2,0:T(8,128)(2,1)S(1)}, u32[]{:S(2)}, u32[]{:S(2)}) collective-permute-start(bf16[1,32,1,6,128]{4,1,3,2,0:T(8,128)(2,1)S(1)} %get-tuple-element.20), channel_id=1, source_target_pairs={{0,2},{1,3},{2,4},{3,5},{4,6},{5,7},{6,8},{7,9},{8,10},{9,11},{10,... | collective-permute-start | bytes 147464 | tf_op jit(solution)/shard_map/ppermute | solution.py:12
  56.0 1.5 collective-permute-start.7
  57.6 2.2 copy.98
  59.7 2.2 copy.99
  61.9 40.1 %pad_maximum_fusion = bf16[1,4,10,10,256]{1,0,4,3,2:T(2,128)(2,1)} fusion(bf16[1,4,1,10,256]{1,0,4,3,2:T(2,128)(2,1)} %copy.99, bf16[1,4,8,1,256]{1,0,4,3,2:T(2,128)(2,1)S(1)} %copy.95, bf16[1,4,8,8,256]{1,0,4,3,2:T(2,128)(2,1)} %copy.94, bf16[1,4,8,1,256]{1,0,4,3,2:T(2,128)(2,1)S(1)} %copy.93, bf16[1,4,1,10,256]{1,0,4,3,2:T(2,128)(2,1)} %copy.98), kind=kLoop, calls=%fused_computation | loop fusion | flops 409600 | bytes 409600 | tf_op jit(solution)/shard_map/concatenate | solution.py:75
  102.0 23.7 %copy.113 = bf16[1,4,10,10,256]{4,1,3,2,0:T(4,128)(2,1)S(1)} copy(bf16[1,4,10,10,256]{1,0,4,3,2:T(2,128)(2,1)} %pad_maximum_fusion) | data formatting | bytes 409600 | tf_op jit(solution)/shard_map/concatenate | solution.py:75
  126.7 4.3 %copy.115 = bf16[4,10,10,1,8,33]{4,0,5,2,1,3:T(4,128)(2,1)} copy(bf16[4,10,10,1,8,33]{5,4,0,2,1,3:T(8,128)(2,1)S(1)} %reshape.57) | data formatting | bytes 422400 | tf_op jit(solution)/shard_map/conv_general_dilated | solution.py:16
  132.1 20.5 %fusion = f32[8,8,8,33,32]{4,2,3,1,0:T(8,128)S(1)} fusion(f32[32]{0:T(128)S(1)} %copy-done.9, pred[8,33]{0,1:T(8,128)(4,1)S(1)} %copy-done.11, bf16[32,4,3,3,3]{0,1,4,3,2:T(4,128)(2,1)S(1)} %copy-done.8, bf16[4,10,10,1,7,2]{4,0,5,2,1,3:T(4,128)(2,1)S(1)} %slice.64, bf16[4,10,10,1,8,33]{4,0,5,2,1,3:T(4,128)(2,1)} %copy.115), kind=kOutput, calls=%fused_computation.2 | convolution fusion | flops 119619840 | bytes 2392392 | tf_op jit(solution)/shard_map/conv_general_dilated | solution.py:16
  152.7 6.0 %copy.121 = f32[8,8,8,33,32]{4,3,2,1,0:T(8,128)} copy(f32[8,8,8,33,32]{4,2,3,1,0:T(8,128)S(1)} %fusion) | data formatting | bytes 4325376 | tf_op jit(solution)/shard_map/jit(_where)/select_n | solution.py:52
  158.7 9.5 %reshape.76 = f32[8,8,1,264,32]{4,3,1,0,2:T(8,128)} reshape(f32[8,8,8,33,32]{4,3,2,1,0:T(8,128)} %copy.121) | data formatting | bytes 4325376 | tf_op jit(solution)/shard_map/jit(_where)/select_n | solution.py:52
  169.1 1.7 reshape.45
  170.9 3.0 copy.103
  174.9 3.5 fusion.53
  181.8 2.0 collective-permute-start.8
  185.8 4.7 %copy.119 = bf16[1,32,6,6,128]{1,0,4,3,2:T(2,128)(2,1)S(1)} copy(bf16[1,32,6,6,128]{4,1,3,2,0:T(8,128)(2,1)} %pad_maximum_fusion.4) | data formatting | bytes 589824 | tf_op jit(solution)/shard_map/concatenate | solution.py:75
  193.4 7.7 %collective-permute-start.10 = (bf16[1,64,1,6,128]{4,1,3,2,0:T(8,128)(2,1)}, bf16[1,64,1,6,128]{4,1,3,2,0:T(8,128)(2,1)S(1)}, u32[]{:S(2)}, u32[]{:S(2)}) collective-permute-start(bf16[1,64,1,6,128]{4,1,3,2,0:T(8,128)(2,1)} %get-tuple-element.18), channel_id=1, source_target_pairs={{0,2},{1,3},{2,4},{3,5},{4,6},{5,7},{6,8},{7,9},{8,10},{9,11},{10,... | collective-permute-start | bytes 294920 | tf_op jit(solution)/shard_map/ppermute | solution.py:12
  202.6 14.7 %fusion.58 = f32[64,32,3,3,3]{0,1,4,3,2:T(8,128)} fusion(bf16[1,32,6,6,128]{1,0,4,3,2:T(2,128)(2,1)S(1)} %copy.119, bf16[1,64,4,4,128]{1,3,4,2,0:T(4,128)(2,1)S(1)} %get-tuple-element.11), kind=kOutput, calls=%fused_computation.50 | convolution fusion | flops 225312768 | bytes 778240 | tf_op jit(solution)/shard_map/transpose | solution.py:35
  220.9 4.3 %fusion.50 = f32[4,4,8,17,32]{4,2,3,1,0:T(8,128)S(1)} fusion(bf16[64,32,3,3,3]{0,1,4,3,2:T(8,128)(2,1)S(1)} %copy-done.7, bf16[64,6,6,1,7,2]{0,4,5,2,1,3:T(8,128)(2,1)S(1)} %slice.62, bf16[64,6,6,1,8,17]{0,4,5,2,1,3:T(8,128)(2,1)S(1)} %copy.110, pred[8,17]{0,1:T(8,128)(4,1)S(1)} %copy-done.12), kind=kOutput, calls=%fused_computation.40 | convolution fusion | flops 243027968 | bytes 1080456 | tf_op jit(solution)/shard_map/conv_general_dilated | solution.py:16
  225.8 7.3 %broadcast_in_dim.41 = f32[32,4,2,4,2,128,2]{0,6,5,4,3,2,1:T(2,128)} broadcast(f32[32,4,4,128]{0,3,2,1:T(8,128)S(1)} %copy.112), dimensions={0,1,3,5} | broadcast | bytes 2359296 | tf_op jit(solution)/shard_map/broadcast_in_dim | solution.py:45
  233.1 9.6 %convert_reduce_fusion = (f32[32]{0:T(128)}, bf16[1,32,8,8,256]{1,4,3,2,0:T(8,128)(2,1)}) fusion(f32[1,32,8,8,256]{1,4,3,2,0:T(8,128)} %bitcast.76, f32[8,8,1,264,32]{4,3,1,0,2:T(8,128)} %reshape.76), kind=kLoop, calls=%fused_computation.6 | loop fusion | flops 2097120 | bytes 5243008 | tf_op jit(solution)/shard_map/reduce_sum | solution.py:88
  242.7 6.3 %all-reduce.5.cloned.1.call-done = f32[64,32,3,3,3]{0,1,4,3,2:T(8,128)} async-done(((f32[64,32,3,3,3]{0,1,4,3,2:T(8,128)}), f32[64,32,3,3,3]{0,1,4,3,2:T(8,128)}) %all-reduce.5.cloned.1.call-update) | async-done | bytes 221200 | tf_op jit(solution)/shard_map/psum | solution.py:114
  249.0 97.4 %fusion.3 = f32[32,4,3,3,3]{0,1,4,3,2:T(4,128)S(1)} fusion(bf16[1,4,10,10,256]{1,0,4,3,2:T(2,128)(2,1)} %pad_maximum_fusion, bf16[1,32,8,8,256]{1,4,3,2,0:T(8,128)(2,1)} %get-tuple-element.13), kind=kOutput, calls=%fused_computation.7 | convolution fusion | flops 112951296 | bytes 1267200 | tf_op jit(solution)/shard_map/transpose | solution.py:35
  346.4 7.6 %all-reduce.1 = (f32[32,4,3,3,3]{0,1,4,3,2:T(4,128)S(1)}, f32[32]{0:T(128)S(1)}, f32[64]{0:T(128)S(1)}) all-reduce(f32[32,4,3,3,3]{0,1,4,3,2:T(4,128)S(1)} %fusion.3, f32[32]{0:T(128)S(1)} %copy-done.4, f32[64]{0:T(128)S(1)} %copy-done.5), channel_id=1, replica_groups=mesh['section'=2,'space'=16] {'section'}, use_global_device_ids=true, to_apply=%region_0.1 | all-reduce | flops 3552 | bytes 28416 | tf_op jit(solution)/shard_map/psum | solution.py:114
  354.0 60.1 %all-reduce = (f32[32,4,3,3,3]{0,1,4,3,2:T(4,128)}, f32[32]{0:T(128)}, f32[64]{0:T(128)}) all-reduce(f32[32,4,3,3,3]{0,1,4,3,2:T(4,128)S(1)} %get-tuple-element.7, f32[32]{0:T(128)S(1)} %get-tuple-element.8, f32[64]{0:T(128)S(1)} %get-tuple-element.9), channel_id=1, replica_groups=mesh['section'=2,'space'=16] {'space'}, use_global_device_ids=true, to_apply=%region_1.2 | all-reduce | flops 3552 | bytes 28416 | tf_op jit(solution)/shard_map/psum | solution.py:115
  414.1 1.8 copy.133
  (84 shorter events, 25.8 us)
Async XLA Ops:
  7.2 1.0 copy-start
  7.2 241.8 %all-reduce.5.cloned.1.call-start = ((), (), s32[]{:S(2)}) async-start(), calls=%async_computation | async-start | bytes 884736 | tf_op jit(solution)/shard_map/psum | solution.py:114
  8.2 21.3 %collective-permute-start = (bf16[1,4,8,1,256]{4,2,3,1,0:T(8,128)(2,1)S(1)}, bf16[1,4,8,1,256]{4,2,3,1,0:T(8,128)(2,1)S(1)}, u32[]{:S(2)}, u32[]{:S(2)}) collective-permute-start(bf16[1,4,8,1,256]{4,2,3,1,0:T(8,128)(2,1)S(1)} %copy.91), channel_id=1, source_target_pairs={{0,1},{1,2},{2,3},{3,4},{4,5},{5,6},{6,7},{7,8},{8,9},{9,10},{10,1... | collective-permute-start | bytes 49160 | tf_op jit(solution)/shard_map/ppermute | solution.py:12
  10.7 19.6 %collective-permute-start.1 = (bf16[1,4,8,1,256]{4,2,3,1,0:T(8,128)(2,1)S(1)}, bf16[1,4,8,1,256]{4,2,3,1,0:T(8,128)(2,1)S(1)}, u32[]{:S(2)}, u32[]{:S(2)}) collective-permute-start(bf16[1,4,8,1,256]{4,2,3,1,0:T(8,128)(2,1)S(1)} %copy.92), channel_id=1, source_target_pairs={{1,0},{2,1},{3,2},{4,3},{5,4},{6,5},{7,6},{8,7},{9,8},{10,9},{11,1... | collective-permute-start | bytes 49160 | tf_op jit(solution)/shard_map/ppermute | solution.py:12
  13.0 37.2 %collective-permute-start.4 = (bf16[1,32,4,1,128]{4,1,3,2,0:T(8,128)(2,1)S(1)}, bf16[1,32,4,1,128]{4,1,3,2,0:T(8,128)(2,1)S(1)}, u32[]{:S(2)}, u32[]{:S(2)}) collective-permute-start(bf16[1,32,4,1,128]{4,1,3,2,0:T(8,128)(2,1)S(1)} %get-tuple-element.22), channel_id=1, source_target_pairs={{0,1},{1,2},{2,3},{3,4},{4,5},{5,6},{6,7},{7,8},{8,9},{9,10},{10,1... | collective-permute-start | bytes 98312 | tf_op jit(solution)/shard_map/ppermute | solution.py:12
  18.1 32.0 %collective-permute-start.5 = (bf16[1,32,4,1,128]{4,1,3,2,0:T(8,128)(2,1)S(1)}, bf16[1,32,4,1,128]{4,1,3,2,0:T(8,128)(2,1)S(1)}, u32[]{:S(2)}, u32[]{:S(2)}) collective-permute-start(bf16[1,32,4,1,128]{4,1,3,2,0:T(8,128)(2,1)S(1)} %get-tuple-element.23), channel_id=1, source_target_pairs={{1,0},{2,1},{3,2},{4,3},{5,4},{6,5},{7,6},{8,7},{9,8},{10,9},{11,1... | collective-permute-start | bytes 98312 | tf_op jit(solution)/shard_map/ppermute | solution.py:12
  40.4 17.1 %collective-permute-start.2 = (bf16[1,4,1,10,256]{4,1,3,2,0:T(4,128)(2,1)S(1)}, bf16[1,4,1,10,256]{4,1,3,2,0:T(4,128)(2,1)S(1)}, u32[]{:S(2)}, u32[]{:S(2)}) collective-permute-start(bf16[1,4,1,10,256]{4,1,3,2,0:T(4,128)(2,1)S(1)} %copy.96), channel_id=1, source_target_pairs={{0,2},{1,3},{2,4},{3,5},{4,6},{5,7},{6,8},{7,9},{8,10},{9,11},{10,... | collective-permute-start | bytes 61448 | tf_op jit(solution)/shard_map/ppermute | solution.py:12
  48.8 10.9 %collective-permute-start.3 = (bf16[1,4,1,10,256]{4,1,3,2,0:T(4,128)(2,1)S(1)}, bf16[1,4,1,10,256]{4,1,3,2,0:T(4,128)(2,1)S(1)}, u32[]{:S(2)}, u32[]{:S(2)}) collective-permute-start(bf16[1,4,1,10,256]{4,1,3,2,0:T(4,128)(2,1)S(1)} %copy.97), channel_id=1, source_target_pairs={{2,0},{3,1},{4,2},{5,3},{6,4},{7,5},{8,6},{9,7},{10,8},{11,9},{12,... | collective-permute-start | bytes 61448 | tf_op jit(solution)/shard_map/ppermute | solution.py:12
  50.2 118.0 %collective-permute-start.6 = (bf16[1,32,1,6,128]{4,1,3,2,0:T(8,128)(2,1)S(1)}, bf16[1,32,1,6,128]{4,1,3,2,0:T(8,128)(2,1)S(1)}, u32[]{:S(2)}, u32[]{:S(2)}) collective-permute-start(bf16[1,32,1,6,128]{4,1,3,2,0:T(8,128)(2,1)S(1)} %get-tuple-element.20), channel_id=1, source_target_pairs={{0,2},{1,3},{2,4},{3,5},{4,6},{5,7},{6,8},{7,9},{8,10},{9,11},{10,... | collective-permute-start | bytes 147464 | tf_op jit(solution)/shard_map/ppermute | solution.py:12
  56.0 112.2 %collective-permute-start.7 = (bf16[1,32,1,6,128]{4,1,3,2,0:T(8,128)(2,1)S(1)}, bf16[1,32,1,6,128]{4,1,3,2,0:T(8,128)(2,1)S(1)}, u32[]{:S(2)}, u32[]{:S(2)}) collective-permute-start(bf16[1,32,1,6,128]{4,1,3,2,0:T(8,128)(2,1)S(1)} %get-tuple-element.21), channel_id=1, source_target_pairs={{2,0},{3,1},{4,2},{5,3},{6,4},{7,5},{8,6},{9,7},{10,8},{11,9},{12,... | collective-permute-start | bytes 147464 | tf_op jit(solution)/shard_map/ppermute | solution.py:12
  126.6 5.4 %copy-start.8 = (bf16[32,4,3,3,3]{0,1,4,3,2:T(4,128)(2,1)S(1)}, bf16[32,4,3,3,3]{0,1,4,3,2:T(4,128)(2,1)}, u32[]{:S(2)}) copy-start(bf16[32,4,3,3,3]{0,1,4,3,2:T(4,128)(2,1)} %param.10) | copy-start | bytes 20740
  126.7 5.4 %copy-start.9 = (f32[32]{0:T(128)S(1)}, f32[32]{0:T(128)}, u32[]{:S(2)}) copy-start(f32[32]{0:T(128)} %param.11) | copy-start | bytes 388
  126.7 5.4 %copy-start.11 = (pred[8,33]{0,1:T(8,128)(4,1)S(1)}, pred[8,33]{0,1:T(8,128)(4,1)}, u32[]{:S(2)}) copy-start(pred[8,33]{0,1:T(8,128)(4,1)} %constant.64) | copy-start | bytes 796
  168.2 0.6 copy-start.2
  170.8 4.0 copy-start.6
  170.8 4.0 copy-start.10
  170.9 4.0 copy-start.12
  179.0 6.1 %copy-start.3 = (bf16[1,32,1,6,128]{4,1,3,2,0:T(8,128)(2,1)S(1)}, bf16[1,32,1,6,128]{4,1,3,2,0:T(8,128)(2,1)}, u32[]{:S(2)}) copy-start(bf16[1,32,1,6,128]{4,1,3,2,0:T(8,128)(2,1)} %copy-done.2) | copy-start | bytes 147460
  181.8 8.8 %collective-permute-start.8 = (bf16[1,64,4,1,128]{1,3,4,2,0:T(2,128)(2,1)}, bf16[1,64,4,1,128]{1,3,4,2,0:T(2,128)(2,1)}, u32[]{:S(2)}, u32[]{:S(2)}) collective-permute-start(bf16[1,64,4,1,128]{1,3,4,2,0:T(2,128)(2,1)} %get-tuple-element.16), channel_id=1, source_target_pairs={{0,1},{1,2},{2,3},{3,4},{4,5},{5,6},{6,7},{7,8},{8,9},{9,10},{10,1... | collective-permute-start | bytes 196616 | tf_op jit(solution)/shard_map/ppermute | solution.py:12
  183.8 7.8 %collective-permute-start.9 = (bf16[1,64,4,1,128]{1,3,4,2,0:T(2,128)(2,1)}, bf16[1,64,4,1,128]{1,3,4,2,0:T(2,128)(2,1)}, u32[]{:S(2)}, u32[]{:S(2)}) collective-permute-start(bf16[1,64,4,1,128]{1,3,4,2,0:T(2,128)(2,1)} %get-tuple-element.17), channel_id=1, source_target_pairs={{1,0},{2,1},{3,2},{4,3},{5,4},{6,5},{7,6},{8,7},{9,8},{10,9},{11,1... | collective-permute-start | bytes 196616 | tf_op jit(solution)/shard_map/ppermute | solution.py:12
  193.4 24.0 %collective-permute-start.10 = (bf16[1,64,1,6,128]{4,1,3,2,0:T(8,128)(2,1)}, bf16[1,64,1,6,128]{4,1,3,2,0:T(8,128)(2,1)S(1)}, u32[]{:S(2)}, u32[]{:S(2)}) collective-permute-start(bf16[1,64,1,6,128]{4,1,3,2,0:T(8,128)(2,1)} %get-tuple-element.18), channel_id=1, source_target_pairs={{0,2},{1,3},{2,4},{3,5},{4,6},{5,7},{6,8},{7,9},{8,10},{9,11},{10,... | collective-permute-start | bytes 294920 | tf_op jit(solution)/shard_map/ppermute | solution.py:12
  201.1 16.3 %collective-permute-start.11 = (bf16[1,64,1,6,128]{4,1,3,2,0:T(8,128)(2,1)S(1)}, bf16[1,64,1,6,128]{4,1,3,2,0:T(8,128)(2,1)}, u32[]{:S(2)}, u32[]{:S(2)}) collective-permute-start(bf16[1,64,1,6,128]{4,1,3,2,0:T(8,128)(2,1)S(1)} %get-tuple-element.19), channel_id=1, source_target_pairs={{2,0},{3,1},{4,2},{5,3},{6,4},{7,5},{8,6},{9,7},{10,8},{11,9},{12,... | collective-permute-start | bytes 294920 | tf_op jit(solution)/shard_map/ppermute | solution.py:12
  217.3 196.8 %all-reduce.7.cloned.1.call-start = ((), (), s32[]{:S(2)}) async-start(), calls=%async_computation.1 | async-start | bytes 884736 | tf_op jit(solution)/shard_map/psum | solution.py:115
  220.0 0.9 copy-start.7
  249.0 97.4 %copy-start.4 = (f32[32]{0:T(128)S(1)}, f32[32]{0:T(128)}, u32[]{:S(2)}) copy-start(f32[32]{0:T(128)} %get-tuple-element.12) | copy-start | bytes 388
  249.0 97.4 %copy-start.5 = (f32[64]{0:T(128)S(1)}, f32[64]{0:T(128)}, u32[]{:S(2)}) copy-start(f32[64]{0:T(128)} %get-tuple-element.10) | copy-start | bytes 772
  249.0 166.9 %copy-start.1 = (bf16[1,2,4,8,8,256]{5,4,3,2,1,0:T(8,128)(2,1)S(1)}, bf16[1,2,4,8,8,256]{5,4,3,2,1,0:T(8,128)(2,1)}, u32[]{:S(2)}) copy-start(bf16[1,2,4,8,8,256]{5,4,3,2,1,0:T(8,128)(2,1)} %param.7) | copy-start | bytes 786436
Sparse Core Ops, SparseCore 0:
  217.4 31.4 all-reduce.4
  252.4 90.4 all-reduce.6
